TPU v7x, 512 devices: a whole 4x4x16 slice. The times are simulated.
512 devices in a mesh: sub: 32 (over z, core), mem: 16 (over x, y).
Axes of the slice: x: 4, y: 4, z: 16, core: 2. Of those that a mesh axis runs over, the one named last changes fastest.
Arguments:
- dechirped_echo_matrix: bfloat16 [32, 2, 256, 8192], P('sub', None, 'mem'), may hold values from -6 to 6
- bearing_rotation_table: float32 [32, 16, 512, 256], P('sub', 'mem'), may hold values from -3.140625 to 3.140625
- patch_subset_holder: int32 [32, 16, 16], P('sub', 'mem'), may hold values from 0 to 31, as said below
- modulation_slope: float32 [32, 16, 2, 16], P('sub', 'mem'), may hold values from -0.5 to 0.5
- regrid_lead_cell: int32 [32, 16, 2, 128], P('sub', 'mem'), may hold values from 0 to 124
- regrid_weight: float32 [32, 16, 2, 128], P('sub', 'mem'), may hold values from 0 to 1
Outputs:
- ground_image: bfloat16 [512, 2, 128, 128], P(('sub', 'mem'))
Inputs may be any that keep to these rules, and one draw needn't show every extreme that they name: `patch_subset_holder`: each group and sector sends at most 2 of its 16 blocks to any one tile; in every sector some tile receives exactly 2 blocks from every group.
All inputs are finite; a program needn't handle non-finite values.
Results may differ from a plain program's by a relative error of at most 0.014.
Values may be sent and summed in bfloat16 or wider, within the bound.
No kernel may reach another device: no remote copies, remote signals or barrier semaphores. Data moves between devices by JAX's collectives and lax.ppermute only.
A program may use at most 64 MiB of HBM per device.

v0:
```python
import math
import jax
import jax.numpy as jnp
from jax import lax
from jax.sharding import PartitionSpec as P

FREQUENCIES = 8192
FIRST_RADIX = 64
SECOND_RADIX = 128
SWEEPS = 256
ANGLES = 512
BLOCK_SIDE = 128


def dft_tables(length):
    positions = jnp.arange(length, dtype=jnp.int32)
    turns = positions[:, None] * positions[None, :] % length
    phase_angle = turns.astype(jnp.float32) * (2.0 * math.pi / length)
    return jnp.stack([jnp.cos(phase_angle), jnp.sin(phase_angle)]).astype(jnp.bfloat16)


def twiddle(row_count, column_count, length):
    row_index = jnp.arange(row_count, dtype=jnp.int32)
    column_index = jnp.arange(column_count, dtype=jnp.int32)
    turns = row_index[:, None] * column_index[None, :] % length
    phase_angle = turns.astype(jnp.float32) * (2.0 * math.pi / length)
    return (jnp.cos(phase_angle), jnp.sin(phase_angle))


def combine(product):
    return (product[0, 0] - product[1, 1], product[0, 1] + product[1, 0])


def range_transform(sweeps):
    sweep_count = sweeps.shape[1]
    reshaped = sweeps.reshape(2, sweep_count, FIRST_RADIX, SECOND_RADIX)
    product = jnp.einsum(
        "qrk,pskj->qpsrj", dft_tables(FIRST_RADIX), reshaped, preferred_element_type=jnp.float32
    )
    inphase_part, quadrature_part = combine(product)
    cosine, sine_part = twiddle(FIRST_RADIX, SECOND_RADIX, FREQUENCIES)
    turned = jnp.stack(
        [
            inphase_part * cosine - quadrature_part * sine_part,
            inphase_part * sine_part + quadrature_part * cosine,
        ]
    ).astype(jnp.bfloat16)
    product = jnp.einsum(
        "quj,psrj->qpsur", dft_tables(SECOND_RADIX), turned, preferred_element_type=jnp.float32
    )
    inphase_part, quadrature_part = combine(product)
    factor = 1.0 / math.sqrt(FREQUENCIES)
    return (
        (jnp.stack([inphase_part, quadrature_part]) * factor)
        .astype(jnp.bfloat16)
        .reshape(2, sweep_count, FREQUENCIES)
    )


def phase_tables(angles):
    factor = 1.0 / math.sqrt(SWEEPS)
    return jnp.stack([jnp.cos(angles) * factor, jnp.sin(angles) * factor]).astype(jnp.bfloat16)


def strip_modulation(
    inphase_part, quadrature_part, modulation_line_entries, tilt_patches, slant_patches
):
    tilt_linear_slope = modulation_line_entries[0].reshape(tilt_patches, slant_patches)
    slant_linear_slope = modulation_line_entries[1].reshape(tilt_patches, slant_patches)
    positions = jnp.arange(BLOCK_SIDE, dtype=jnp.float32)
    phase_angle = (
        tilt_linear_slope[:, None, :, None] * positions[None, :, None, None]
        + slant_linear_slope[:, None, :, None] * positions[None, None, None, :]
    )
    cosine = jnp.cos(phase_angle)
    sine_part = jnp.sin(phase_angle)
    inphase_part = inphase_part.reshape(tilt_patches, BLOCK_SIDE, slant_patches, BLOCK_SIDE)
    quadrature_part = quadrature_part.reshape(tilt_patches, BLOCK_SIDE, slant_patches, BLOCK_SIDE)
    return jnp.stack(
        [
            inphase_part * cosine - quadrature_part * sine_part,
            inphase_part * sine_part + quadrature_part * cosine,
        ]
    ).astype(jnp.bfloat16)


def stencil(offsets, fractions):
    weights = [
        -fractions * (fractions - 1.0) * (fractions - 2.0) / 6.0,
        (fractions + 1.0) * (fractions - 1.0) * (fractions - 2.0) / 2.0,
        -(fractions + 1.0) * fractions * (fractions - 2.0) / 2.0,
        (fractions + 1.0) * fractions * (fractions - 1.0) / 6.0,
    ]
    sources = jnp.arange(fractions.shape[-1], dtype=jnp.int32)
    distance = sources - offsets[..., None]
    weights_sum = jnp.zeros(distance.shape, jnp.float32)
    for stencil_tap in range(4):
        weights_sum = weights_sum + jnp.where(
            distance == stencil_tap, weights[stencil_tap][..., None], jnp.float32(0.0)
        )
    return weights_sum.astype(jnp.bfloat16)


def on_device(
    dechirped_echo_matrix,
    bearing_rotation_table,
    patch_subset_holder,
    modulation_slope,
    regrid_lead_cell,
    regrid_weight,
):
    groups = lax.axis_size("sub")
    members = lax.axis_size("mem")
    sector = FREQUENCIES // members
    tilt_patches = ANGLES // BLOCK_SIDE
    slant_patches = sector // BLOCK_SIDE
    block_count = tilt_patches * slant_patches
    capacity = max(2, 2 * block_count // groups)
    spectrum = range_transform(dechirped_echo_matrix[0])
    sweep_count = spectrum.shape[1]
    by_sector = spectrum.reshape(2, sweep_count, members, sector)
    tables = phase_tables(bearing_rotation_table[0, 0])
    product = jnp.einsum(
        "qas,psc->qpac",
        tables,
        lax.all_to_all(by_sector, "mem", split_axis=2, concat_axis=1, tiled=True)[:, :, 0, :],
        preferred_element_type=jnp.float32,
    )
    inphase_part, quadrature_part = combine(product)
    focused_image = jnp.stack([inphase_part, quadrature_part])[:, :, None, :]
    patch_list = strip_modulation(
        focused_image[0, :, 0, :],
        focused_image[1, :, 0, :],
        modulation_slope[0, 0],
        tilt_patches,
        slant_patches,
    )
    own_tables = stencil(regrid_lead_cell[0, 0], regrid_weight[0, 0])
    owners = patch_subset_holder[0, 0]
    onehot = owners[:, None] == jnp.arange(groups, dtype=jnp.int32)[None, :]
    counts = onehot.astype(jnp.int32)
    before = jnp.cumsum(counts, axis=0) - counts
    rank_within = jnp.sum(before * counts, axis=1)
    slot_index = owners * capacity + rank_within
    selector = (
        slot_index[None, :] == jnp.arange(groups * capacity, dtype=jnp.int32)[:, None]
    ).astype(jnp.bfloat16)
    selector = selector.reshape(groups * capacity, tilt_patches, slant_patches)
    packed = jnp.einsum(
        "kAC,pAaCc->kpac", selector, patch_list, preferred_element_type=jnp.float32
    ).astype(jnp.bfloat16)
    packed = packed.reshape(groups, capacity, 2, BLOCK_SIDE, BLOCK_SIDE)
    rows_done = jnp.einsum(
        "ya,skpac->skpyc",
        own_tables[0],
        lax.all_to_all(packed, "sub", split_axis=0, concat_axis=0, tiled=True),
        preferred_element_type=jnp.float32,
    ).astype(jnp.bfloat16)
    interpolated = jnp.einsum(
        "skpyc,xc->skpyx", rows_done, own_tables[1], preferred_element_type=jnp.float32
    )
    per_source = lax.optimization_barrier(jnp.sum(interpolated, axis=1).astype(jnp.bfloat16))
    ground = jnp.sum(per_source.astype(jnp.float32), axis=0)
    return (0.25 * ground).astype(jnp.bfloat16)[None]


def solution(mesh):
    return jax.shard_map(
        on_device,
        mesh=mesh,
        in_specs=(
            P("sub", None, "mem", None),
            P("sub", "mem", None, None),
            P("sub", "mem", None),
            P("sub", "mem", None, None),
            P("sub", "mem", None, None),
            P("sub", "mem", None, None),
        ),
        out_specs=P(("sub", "mem"), None, None, None),
        check_vma=False,
    )
```

profile of v0, /device:TPU:32, one launch (start us, length us, event | category | flops | bytes accessed | tf_op | source)
XLA Modules:
  0.0 251.5 jit_solution(1296951972144069994)
XLA Ops:
  0.0 0.2 sine_convert_fusion.1
  0.2 0.1 fusion.59
  0.3 0.3 sine_convert_fusion
  0.6 1.2 copy.78
  1.8 0.4 convolution_bitcast_fusion.2
  2.2 0.2 subtract_convert_fusion
  2.4 0.4 convolution_bitcast_fusion.1
  2.8 0.2 slice_subtract_fusion.1
  3.0 0.3 copy.53
  3.4 0.0 copy-start.4
  3.4 0.0 copy-start.1
  3.4 0.0 copy-start
  3.4 0.3 add.211
  3.7 0.3 copy.52
  4.0 0.3 sub.102
  4.3 0.1 fusion.22
  4.4 1.1 copy.54
  5.5 7.0 %all-to-all-start = ((bf16[2,16,16,512]{3,1,0,2:T(8,128)(2,1)}), bf16[2,16,16,512]{3,1,0,2:T(8,128)(2,1)S(1)}, u32[]{:S(2)}, u32[]{:S(2)}) async-start(bf16[2,16,16,512]{3,1,0,2:T(8,128)(2,1)} %copy.54), calls=%async_computation | async-start | bytes 1048576 | tf_op jit(solution)/shard_map/all_to_all | solution.py:126
  12.6 0.0 copy-done.4
  12.6 0.1 mul.445
  12.7 0.1 iota_multiply_fusion
  12.8 0.0 copy-done.1
  12.8 0.1 fusion.61
  12.9 0.2 select_reduce_fusion
  13.1 0.1 mul.441
  13.2 0.1 reduce_sum.30
  13.2 0.1 mul.412
  13.3 0.1 iota_multiply_fusion.1
  13.4 0.0 copy-done
  13.4 1.9 fusion.30
  15.3 8.7 %all-to-all-done = bf16[2,16,16,512]{3,1,0,2:T(8,128)(2,1)S(1)} async-done(((bf16[2,16,16,512]{3,1,0,2:T(8,128)(2,1)}), bf16[2,16,16,512]{3,1,0,2:T(8,128)(2,1)S(1)}, u32[]{:S(2)}, u32[]{:S(2)}) %all-to-all-start) | async-done | bytes 524320 | tf_op jit(solution)/shard_map/all_to_all | solution.py:126
  24.1 0.8 convolution_bitcast_fusion
  24.9 0.5 slice_subtract_fusion
  25.3 0.8 copy.57
  26.1 0.8 copy.59
  26.9 4.6 %fusion.19 = (bf16[1,4,128,4,128]{4,2,3,1,0:T(8,128)(2,1)S(1)}, bf16[1,4,128,4,128]{4,2,3,1,0:T(8,128)(2,1)S(1)}) fusion(f32[1,4,128,4,128]{4,3,0,2,1:T(4,128)S(1)} %bitcast.122, f32[1,4,128,4,128]{4,3,0,2,1:T(4,128)S(1)} %bitcast.121, f32[4,4,128]{2,1,0:T(4,128)S(1)} %iota_multiply_fusion, f32[4,128,4]{1,2,0:T(4,128)S(1)} %iota_multiply_fusion.1), kind=kLoop, calls=%fused_computation.18 | loop fusion | flops 2359296 | bytes 3162112 | tf_op jit(solution)/shard_map/convert
  31.6 0.1 pad_maximum_fusion
  31.7 1.9 bitcast_convert_fusion
  33.6 6.6 %copy.64 = bf16[32,2,2,128,128]{4,1,3,2,0:T(2,128)(2,1)} copy(bf16[32,2,2,128,128]{4,1,0,3,2:T(2,128)(2,1)S(1)} %bitcast.123) | data formatting | bytes 8388608 | tf_op jit(solution)/shard_map/reshape | solution.py:152
  40.2 0.0 copy-start.3
  40.2 15.5 %all-to-all-start.1 = ((bf16[32,2,2,128,128]{4,1,3,2,0:T(2,128)(2,1)}), bf16[32,2,2,128,128]{4,1,3,2,0:T(2,128)(2,1)}, u32[]{:S(2)}, u32[]{:S(2)}) async-start(bf16[32,2,2,128,128]{4,1,3,2,0:T(2,128)(2,1)} %copy.64), calls=%async_computation.1 | async-start | bytes 8388608 | tf_op jit(solution)/shard_map/all_to_all | solution.py:156
  55.8 0.0 copy-done.3
  55.8 0.0 copy-done.2
  55.8 0.2 add_convert_fusion.1
  56.0 189.5 %all-to-all-done.1 = bf16[32,2,2,128,128]{4,1,3,2,0:T(2,128)(2,1)} async-done(((bf16[32,2,2,128,128]{4,1,3,2,0:T(2,128)(2,1)}), bf16[32,2,2,128,128]{4,1,3,2,0:T(2,128)(2,1)}, u32[]{:S(2)}, u32[]{:S(2)}) %all-to-all-start.1) | async-done | bytes 4194336 | tf_op jit(solution)/shard_map/all_to_all | solution.py:156
  245.5 5.0 %fusion.9 = bf16[32,2,128,128]{3,2,1,0:T(8,128)(2,1)S(1)} fusion(bf16[32,2,2,128,128]{4,1,3,2,0:T(2,128)(2,1)} %all-to-all-done.1, bf16[2,128,128]{2,1,0:T(8,128)(2,1)S(1)} %add_convert_fusion.1), kind=kOutput, calls=%fused_computation.7 | convolution fusion | flops 1076887552 | bytes 6356992 | tf_op jit(solution)/shard_map/skpyc,xc->skpyx/dot_general | solution.py:159
  250.5 0.3 convert_reduce_fusion
  250.8 0.6 fusion.39
  (7 shorter events, 0.1 us)
Async XLA Ops:
  3.4 9.2 %copy-start.4 = (f32[1,1,2,16]{3,2,1,0:T(2,128)S(1)}, f32[1,1,2,16]{3,2,1,0:T(2,128)}, u32[]{:S(2)}) copy-start(f32[1,1,2,16]{3,2,1,0:T(2,128)} %param.9) | copy-start | bytes 388
  3.4 9.4 %copy-start.1 = (s32[1,1,16]{2,1,0:T(1,128)S(1)}, s32[1,1,16]{2,1,0:T(1,128)}, u32[]{:S(2)}) copy-start(s32[1,1,16]{2,1,0:T(1,128)} %param.8) | copy-start | bytes 196
  3.4 10.0 %copy-start = (f32[1,1,512,256]{3,2,1,0:T(8,128)S(1)}, f32[1,1,512,256]{3,2,1,0:T(8,128)}, u32[]{:S(2)}) copy-start(f32[1,1,512,256]{3,2,1,0:T(8,128)} %param.7) | copy-start | bytes 1572868
  5.5 18.5 %all-to-all-start = ((bf16[2,16,16,512]{3,1,0,2:T(8,128)(2,1)}), bf16[2,16,16,512]{3,1,0,2:T(8,128)(2,1)S(1)}, u32[]{:S(2)}, u32[]{:S(2)}) async-start(bf16[2,16,16,512]{3,1,0,2:T(8,128)(2,1)} %copy.54), calls=%async_computation | async-start | bytes 1048576 | tf_op jit(solution)/shard_map/all_to_all | solution.py:126
  40.2 15.6 %copy-start.3 = (f32[1,1,2,128]{3,2,1,0:T(2,128)S(1)}, f32[1,1,2,128]{3,2,1,0:T(2,128)}, u32[]{:S(2)}) copy-start(f32[1,1,2,128]{3,2,1,0:T(2,128)} %param.11) | copy-start | bytes 3076
  40.2 15.6 %copy-start.2 = (s32[1,1,2,128]{3,2,1,0:T(2,128)S(1)}, s32[1,1,2,128]{3,2,1,0:T(2,128)}, u32[]{:S(2)}) copy-start(s32[1,1,2,128]{3,2,1,0:T(2,128)} %param.10) | copy-start | bytes 3076
  40.2 205.3 %all-to-all-start.1 = ((bf16[32,2,2,128,128]{4,1,3,2,0:T(2,128)(2,1)}), bf16[32,2,2,128,128]{4,1,3,2,0:T(2,128)(2,1)}, u32[]{:S(2)}, u32[]{:S(2)}) async-start(bf16[32,2,2,128,128]{4,1,3,2,0:T(2,128)(2,1)} %copy.64), calls=%async_computation.1 | async-start | bytes 8388608 | tf_op jit(solution)/shard_map/all_to_all | solution.py:156
where the time goes:
time: 252 us; the launch traced here: 251 us
  waiting for transfers between devices  198 us (79%)
  starting transfers between devices  22.6 us (9%)
  local copies, waits for them, and re-layouts  12.1 us (5%)
  other arithmetic  9.92 us (4%)
  matrix products  8.43 us (3%)
    all_to_all x1, waiting for transfers between devices, on_device(): lax.all_to_all(packed, 'sub', split_axis=0, concat_axis=0, tiled=True)  189 us
    all_to_all x1, starting transfers between devices, on_device(): lax.all_to_all(packed, 'sub', split_axis=0, concat_axis=0, tiled=True)  15.5 us
    all_to_all x1, waiting for transfers between devices, on_device(): lax.all_to_all(by_sector, 'mem', split_axis=2, concat_axis=1, tiled=True)  8.73 us
    all_to_all x1, starting transfers between devices, on_device(): lax.all_to_all(by_sector, 'mem', split_axis=2, concat_axis=1, tiled=True)  7.04 us
    reshape x1, local copies, waits for them, and re-layouts, on_device(): packed = packed.reshape(groups, capacity, 2, BLOCK_SIDE, BLOCK_SIDE)  6.62 us
    another operation x4, other arithmetic  5.31 us
  transfers between devices with their start and end apart: 2, of which 2 were waited for; matrix products, arithmetic and copies ran while one was open for 1% of the time, Pallas kernels for 0%

commit v1 on v0

--- a/solution.py
+++ b/solution.py
@@ -1,3 +1,4 @@
+import functools
 import math
 import jax
 import jax.numpy as jnp
@@ -10,6 +11,21 @@
 SWEEPS = 256
 ANGLES = 512
 BLOCK_SIDE = 128
+
+
+def shape_the_sheet(local_x, net_axis):
+    return jnp.concatenate(
+        lax.all_to_all(
+            jnp.stack(jnp.split(local_x, lax.axis_size(net_axis), 2), axis=0),
+            split_axis=0,
+            axis_name=net_axis,
+            concat_axis=0,
+        ),
+        axis=1,
+    )
+
+
+advance_ladders_here = functools.partial(shape_the_sheet, net_axis="mem")
 
 
 def dft_tables(length):
@@ -123,7 +139,7 @@
     product = jnp.einsum(
         "qas,psc->qpac",
         tables,
-        lax.all_to_all(by_sector, "mem", split_axis=2, concat_axis=1, tiled=True)[:, :, 0, :],
+        advance_ladders_here(by_sector)[:, :, 0, :],
         preferred_element_type=jnp.float32,
     )
     inphase_part, quadrature_part = combine(product)

time: 252 us -> 268 us (1.063)
  local copies, waits for them, and re-layouts: 12.1 us -> 26.6 us
    unnamed x11 -> x26, local copies, waits for them, and re-layouts: 1.18 us -> 10.3 us
    reshape x1, local copies, waits for them, and re-layouts: 6.62 us -> 11.4 us  [on_device(): packed = packed.reshape(groups, capacity, 2, BLOCK_SIDE, BLOCK_SIDE)]
where the time goes in v1:
time: 268 us
  waiting for transfers between devices  198 us (74%)
  local copies, waits for them, and re-layouts  26.6 us (10%)
  starting transfers between devices  22.6 us (8%)
  matrix products  10.3 us (4%)
  other arithmetic  9.92 us (4%)
    all_to_all x1, waiting for transfers between devices, on_device(): lax.all_to_all(packed, 'sub', split_axis=0, concat_axis=0, tiled=True)  189 us
    all_to_all x1, starting transfers between devices, on_device(): lax.all_to_all(packed, 'sub', split_axis=0, concat_axis=0, tiled=True)  15.5 us
    reshape x1, local copies, waits for them, and re-layouts, on_device(): packed = packed.reshape(groups, capacity, 2, BLOCK_SIDE, BLOCK_SIDE)  11.4 us
    unnamed x26, local copies, waits for them, and re-layouts  10.3 us
    all_to_all x1, waiting for transfers between devices, shape_the_sheet(): lax.all_to_all(jnp.stack(jnp.split(local_x, lax.axis_size(net_axis), 2),...  8.74 us
    all_to_all x1, starting transfers between devices, shape_the_sheet(): lax.all_to_all(jnp.stack(jnp.split(local_x, lax.axis_size(net_axis), 2),...  7.04 us
  transfers between devices with their start and end apart: 2, of which 2 were waited for; matrix products, arithmetic and copies ran while one was open for 1% of the time, Pallas kernels for 0%

profile of v1, /device:TPU:32, one launch (start us, length us, event | category | flops | bytes accessed | tf_op | source)
XLA Modules:
  0.0 267.9 jit_solution(12341329965060275157)
XLA Ops:
  0.0 0.2 sine_convert_fusion.1
  0.2 0.1 fusion.53
  0.3 0.3 sine_convert_fusion
  0.6 1.2 copy.346
  1.8 0.4 convolution_bitcast_fusion.2
  2.2 0.2 subtract_convert_fusion
  2.4 0.4 convolution_bitcast_fusion.1
  2.8 0.2 slice_subtract_fusion.1
  3.0 0.3 copy.307
  3.4 0.3 add.211
  3.6 0.3 copy.306
  4.0 0.3 sub.102
  4.3 0.1 fusion.16
  4.4 1.1 fusion.72
  5.6 0.6 constant_dynamic-update-slice_fusion.15
  6.2 0.6 constant_dynamic-update-slice_fusion.14
  6.8 0.6 constant_dynamic-update-slice_fusion.13
  7.4 0.6 constant_dynamic-update-slice_fusion.12
  8.0 0.6 constant_dynamic-update-slice_fusion.11
  8.6 0.6 constant_dynamic-update-slice_fusion.10
  9.2 0.6 constant_dynamic-update-slice_fusion.9
  9.8 0.6 constant_dynamic-update-slice_fusion.8
  10.5 0.6 constant_dynamic-update-slice_fusion.7
  11.1 0.6 constant_dynamic-update-slice_fusion.6
  11.7 0.6 constant_dynamic-update-slice_fusion.5
  12.3 0.6 constant_dynamic-update-slice_fusion.4
  12.9 0.6 constant_dynamic-update-slice_fusion.3
  13.5 0.6 constant_dynamic-update-slice_fusion.2
  14.1 0.6 constant_dynamic-update-slice_fusion.1
  14.7 0.6 constant_dynamic-update-slice_fusion
  15.3 7.0 %all-to-all-start = ((bf16[16,2,16,1,512]{4,2,1,3,0:T(8,128)(2,1)}), bf16[16,2,16,1,512]{4,2,1,3,0:T(8,128)(2,1)S(1)}, u32[]{:S(2)}, u32[]{:S(2)}) async-start(bf16[16,2,16,1,512]{4,2,1,3,0:T(8,128)(2,1)} %constant_dynamic-update-slice_fusion), calls=%async_computation | async-start | bytes 1048576 | tf_op jit(solution)/shard_map/all_to_all | solution.py:18
  22.7 0.2 select_reduce_fusion
  23.2 1.9 fusion.24
  25.1 8.7 %all-to-all-done = bf16[16,2,16,1,512]{4,2,1,3,0:T(8,128)(2,1)S(1)} async-done(((bf16[16,2,16,1,512]{4,2,1,3,0:T(8,128)(2,1)}), bf16[16,2,16,1,512]{4,2,1,3,0:T(8,128)(2,1)S(1)}, u32[]{:S(2)}, u32[]{:S(2)}) %all-to-all-start) | async-done | bytes 524320 | tf_op jit(solution)/shard_map/all_to_all | solution.py:18
  33.9 0.8 convolution_bitcast_fusion
  34.7 0.5 slice_subtract_fusion
  35.2 0.8 copy.310
  36.0 0.8 copy.312
  36.8 4.6 %fusion.13 = (bf16[1,4,128,4,128]{4,2,3,1,0:T(8,128)(2,1)S(1)}, bf16[1,4,128,4,128]{4,2,3,1,0:T(8,128)(2,1)S(1)}) fusion(f32[1,4,128,4,128]{4,3,0,2,1:T(4,128)S(1)} %bitcast.152, f32[1,4,128,4,128]{4,3,0,2,1:T(4,128)S(1)} %bitcast.151, f32[4,4,128]{2,1,0:T(4,128)S(1)} %iota_multiply_fusion, f32[4,128,4]{1,2,0:T(4,128)S(1)} %iota_multiply_fusion.1), kind=kLoop, calls=%fused_computation.17 | loop fusion | flops 2359296 | bytes 3162112 | tf_op jit(solution)/shard_map/convert
  41.4 0.1 pad_maximum_fusion
  41.5 3.8 %bitcast_convert_fusion = bf16[64,2,128,128]{3,0,2,1:T(8,128)(2,1)} fusion(bf16[2,4,128,4,128]{4,2,3,1,0:T(8,128)(2,1)S(1)} %pad_maximum_fusion, s32[4,4]{1,0:T(4,128)S(1)} %add.203), kind=kOutput, calls=%fused_computation | convolution fusion | flops 69207040 | bytes 5242944 | tf_op jit(solution)/shard_map/kAC,pAaCc->kpac/dot_general | solution.py:165
  45.4 11.4 %copy.317 = bf16[32,2,2,128,128]{3,4,2,1,0:T(8,128)(2,1)} copy(bf16[32,2,2,128,128]{4,1,0,3,2:T(2,128)(2,1)} %bitcast.153) | data formatting | bytes 8388608 | tf_op jit(solution)/shard_map/reshape | solution.py:168
  56.7 15.5 %all-to-all-start.1 = ((bf16[32,2,2,128,128]{3,4,2,1,0:T(8,128)(2,1)}), bf16[32,2,2,128,128]{3,4,2,1,0:T(8,128)(2,1)}, u32[]{:S(2)}, u32[]{:S(2)}) async-start(bf16[32,2,2,128,128]{3,4,2,1,0:T(8,128)(2,1)} %copy.317), calls=%async_computation.1 | async-start | bytes 8388608 | tf_op jit(solution)/shard_map/all_to_all | solution.py:172
  72.3 0.2 add_convert_fusion.1
  72.5 189.5 %all-to-all-done.1 = bf16[32,2,2,128,128]{3,4,2,1,0:T(8,128)(2,1)} async-done(((bf16[32,2,2,128,128]{3,4,2,1,0:T(8,128)(2,1)}), bf16[32,2,2,128,128]{3,4,2,1,0:T(8,128)(2,1)}, u32[]{:S(2)}, u32[]{:S(2)}) %all-to-all-start.1) | async-done | bytes 4194336 | tf_op jit(solution)/shard_map/all_to_all | solution.py:172
  262.0 4.9 %fusion.5 = bf16[32,2,128,128]{3,2,1,0:T(8,128)(2,1)S(1)} fusion(bf16[32,2,2,128,128]{3,4,2,1,0:T(8,128)(2,1)} %all-to-all-done.1, bf16[2,128,128]{2,1,0:T(8,128)(2,1)S(1)} %add_convert_fusion.1), kind=kOutput, calls=%fused_computation.6 | convolution fusion | flops 1076887552 | bytes 6356992 | tf_op jit(solution)/shard_map/skpyc,xc->skpyx/dot_general | solution.py:175
  266.9 0.3 convert_reduce_fusion
  267.3 0.6 fusion.33
  (23 shorter events, 0.7 us)
Async XLA Ops:
  4.0 18.4 %copy-start.4 = (f32[1,1,2,16]{3,2,1,0:T(2,128)S(1)}, f32[1,1,2,16]{3,2,1,0:T(2,128)}, u32[]{:S(2)}) copy-start(f32[1,1,2,16]{3,2,1,0:T(2,128)} %param.9) | copy-start | bytes 388
  4.0 18.6 %copy-start.1 = (s32[1,1,16]{2,1,0:T(1,128)S(1)}, s32[1,1,16]{2,1,0:T(1,128)}, u32[]{:S(2)}) copy-start(s32[1,1,16]{2,1,0:T(1,128)} %param.8) | copy-start | bytes 196
  4.0 19.2 %copy-start = (f32[1,1,512,256]{3,2,1,0:T(8,128)S(1)}, f32[1,1,512,256]{3,2,1,0:T(8,128)}, u32[]{:S(2)}) copy-start(f32[1,1,512,256]{3,2,1,0:T(8,128)} %param.7) | copy-start | bytes 1572868
  15.3 18.5 %all-to-all-start = ((bf16[16,2,16,1,512]{4,2,1,3,0:T(8,128)(2,1)}), bf16[16,2,16,1,512]{4,2,1,3,0:T(8,128)(2,1)S(1)}, u32[]{:S(2)}, u32[]{:S(2)}) async-start(bf16[16,2,16,1,512]{4,2,1,3,0:T(8,128)(2,1)} %constant_dynamic-update-slice_fusion), calls=%async_computation | async-start | bytes 1048576 | tf_op jit(solution)/shard_map/all_to_all | solution.py:18
  56.7 15.5 %copy-start.3 = (f32[1,1,2,128]{3,2,1,0:T(2,128)S(1)}, f32[1,1,2,128]{3,2,1,0:T(2,128)}, u32[]{:S(2)}) copy-start(f32[1,1,2,128]{3,2,1,0:T(2,128)} %param.11) | copy-start | bytes 3076
  56.7 15.6 %copy-start.2 = (s32[1,1,2,128]{3,2,1,0:T(2,128)S(1)}, s32[1,1,2,128]{3,2,1,0:T(2,128)}, u32[]{:S(2)}) copy-start(s32[1,1,2,128]{3,2,1,0:T(2,128)} %param.10) | copy-start | bytes 3076
  56.7 205.3 %all-to-all-start.1 = ((bf16[32,2,2,128,128]{3,4,2,1,0:T(8,128)(2,1)}), bf16[32,2,2,128,128]{3,4,2,1,0:T(8,128)(2,1)}, u32[]{:S(2)}, u32[]{:S(2)}) async-start(bf16[32,2,2,128,128]{3,4,2,1,0:T(8,128)(2,1)} %copy.317), calls=%async_computation.1 | async-start | bytes 8388608 | tf_op jit(solution)/shard_map/all_to_all | solution.py:172
